TPU v7x, 32 devices: a whole 2x2x4 slice. The times are simulated.
32 devices in a mesh: jpair: 2 (over x), blk: 16 (over z, y, core).
Axes of the slice: x: 2, y: 2, z: 4, core: 2. Of those that a mesh axis runs over, the one named last changes fastest.
Arguments:
- dipole: bfloat16 [256, 12, 3, 256, 256], P('blk'), may hold values from -24 to 24
- block_cols: int32 [256, 12], P('blk'), may hold values from 0 to 255, as said below
- upper_vecs: bfloat16 [131072, 256], P(('jpair', 'blk')), parts along dimension 0, may hold values from -0.0234375 to 0.0234375
- lower_vecs: bfloat16 [131072, 128], P(('jpair', 'blk')), parts along dimension 0, may hold values from -0.0234375 to 0.0234375
- upper_energy: float32 [512], P('jpair'), parts along dimension 0, may hold values from 1 to 2
- lower_energy: float32 [256], P('jpair'), parts along dimension 0, may hold values from 0 to 0.8
Outputs:
- strength: float32 [512, 128], P(('jpair', 'blk')), parts along dimension 0
- intensity: float32 [512, 128], P(('jpair', 'blk')), parts along dimension 0
There are 2 independent parts, one for each index of `jpair`. A program takes and returns all parts, laid end to end along the dimension named above; an argument that names none is the same for every part. Nothing has to cross between parts.
Inputs may be any that keep to these rules, and one draw needn't show every extreme that they name: `block_cols`: within one block row the 12 block columns are distinct, and one of them is the row's own index. Splitting the block rows into 16 equal runs of consecutive rows, the columns of one run that fall in another run number at most 12 distinct blocks for each other run, and exactly 12 for some.
All inputs are finite; a program needn't handle non-finite values.
Results may differ from a plain program's by a relative error of at most 0.0026.
Values may be sent and summed in bfloat16 or wider, within the bound.
A program may use at most 256 MiB of HBM per device.

v0:
```python
import jax
import jax.numpy as jnp
from jax import lax
from jax.sharding import PartitionSpec as P

THERMAL = 0.3


def per_device(dipole, block_cols, upper_vecs, lower_vecs, upper_energy, lower_energy):
    rows_blk, nonzero, n_comps, block_size, _ = dipole.shape
    upper_count = upper_vecs.shape[1]
    lower_count = lower_vecs.shape[1]
    upper_blocks = upper_vecs.reshape(rows_blk, block_size, upper_count)
    halves = jnp.einsum(
        "rkast,rsu->rkatu", dipole, upper_blocks, preferred_element_type=jnp.float32
    ).astype(jnp.bfloat16)
    entry_count = rows_blk * nonzero
    halves = halves.reshape(entry_count, n_comps, block_size, upper_count)
    columns = block_cols.reshape(entry_count)
    group_size = lax.axis_size("blk")
    my_index = lax.axis_index("blk")
    gathered = lax.all_gather(lower_vecs, "blk", axis=0, tiled=True)
    all_blocks = gathered.reshape(gathered.shape[0] // block_size, block_size, lower_count)
    lows = jnp.take(all_blocks, columns, axis=0)
    proj = jnp.einsum("eatu,etl->aul", halves, lows, preferred_element_type=jnp.float32)
    share_rows = upper_count // group_size
    first_row = my_index * share_rows
    summed = lax.psum(proj, "blk")
    own_share = lax.dynamic_slice_in_dim(summed, first_row, share_rows, 1)
    strength = jnp.sum(own_share * own_share, axis=0)
    energy_rows = lax.dynamic_slice_in_dim(upper_energy, first_row, share_rows, 0)
    wavenumber = energy_rows[:, None] - lower_energy[None, :]
    intensity = wavenumber**3 * jnp.exp(-lower_energy / THERMAL)[None, :] * strength
    return (strength, intensity)


def solution(mesh):
    placed = (
        P("blk", None, None, None, None),
        P("blk", None),
        P(("jpair", "blk"), None),
        P(("jpair", "blk"), None),
        P("jpair"),
        P("jpair"),
    )
    return jax.shard_map(
        per_device,
        mesh=mesh,
        in_specs=placed,
        out_specs=(P(("jpair", "blk"), None), P(("jpair", "blk"), None)),
        check_vma=False,
    )
```

profile of v0, /device:TPU:0, one launch (start us, length us, event | category | flops | bytes accessed | tf_op | source)
XLA Modules:
  0.0 283.5 jit_solution(16496702931421474902)
XLA Ops:
  7.2 0.0 copy-start
  7.2 0.0 all-gather.2.cloned.1.call-start
  7.2 0.7 all-gather.2.cloned.1.call-update
  7.9 0.0 all-reduce.2.cloned.1.call-start
  8.0 0.8 reshape.59
  8.8 0.8 reshape.57
  9.5 0.8 dynamic_slice.7
  10.3 0.0 copy-done
  10.3 59.0 %convolution_convert_fusion = bf16[16,12,3,256,256]{4,3,2,1,0:T(8,128)(2,1)} fusion(bf16[16,12,3,256,256]{4,3,2,1,0:T(8,128)(2,1)} %param.6, bf16[16,256,256,1,1]{2,1,4,3,0:T(8,128)(2,1)S(1)} %bitcast.20), kind=kOutput, calls=%fused_computation.1 | convolution fusion | flops 19365101568 | bytes 153092096 | tf_op jit(solution)/shard_map/rkast,rsu->rkatu/dot_general | solution.py:14
  69.4 70.4 %all-gather.2.cloned.1.call-done = bf16[65536,128]{1,0:T(8,128)(2,1)} async-done(((bf16[4096,128]{1,0:T(8,128)(2,1)}), bf16[65536,128]{1,0:T(8,128)(2,1)}) %all-gather.2.cloned.1.call-update) | async-done | bytes 16777232 | tf_op jit(solution)/shard_map/all_gather | solution.py:22
  139.8 13.9 %gather_fusion = bf16[192,256,128]{2,1,0:T(8,128)(2,1)} fusion(bf16[256,256,128]{2,1,0:T(8,128)(2,1)} %bitcast.21, s32[1024]{0:T(1024)S(1)} %pad_clamp_fusion), kind=kCustom, calls=%fused_computation | custom fusion | bytes 25166592 | tf_op jit(solution)/shard_map/jit(_take)/gather | solution.py:24
  153.7 0.0 copy-start.2
  153.8 32.8 %fusion.5 = f32[3,256,128]{2,1,0:T(8,128)} fusion(bf16[192,3,256,256]{3,2,1,0:T(8,128)(2,1)} %bitcast.3, bf16[192,256,128]{2,1,0:T(8,128)(2,1)} %gather_fusion, pred[192]{0:T(512)(128)(4,1)S(1)} %compare_and_fusion), kind=kOutput, calls=%fused_computation.7 | convolution fusion | flops 9669967872 | bytes 88473792 | tf_op jit(solution)/shard_map/eatu,etl->aul/dot_general | solution.py:25
  186.6 0.0 all-reduce.2.cloned.1.call-update
  186.6 0.0 copy-done.2
  186.6 88.6 %all-reduce.2.cloned.1.call-done = f32[3,256,128]{2,1,0:T(8,128)} async-done(((f32[3,256,128]{2,1,0:T(8,128)}), f32[3,256,128]{2,1,0:T(8,128)}) %all-reduce.2.cloned.1.call-update) | async-done | bytes 393232 | tf_op jit(solution)/shard_map/psum | solution.py:28
  275.2 0.7 multiply_reduce_fusion
  276.0 0.0 copy-start.1
  276.0 0.7 fusion.9
  276.7 0.0 copy-done.1
  (4 shorter events, 0.0 us)
Async XLA Ops:
  7.2 3.2 %copy-start = (bf16[4096,256]{1,0:T(8,128)(2,1)S(1)}, bf16[4096,256]{1,0:T(8,128)(2,1)}, u32[]{:S(2)}) copy-start(bf16[4096,256]{1,0:T(8,128)(2,1)} %param.8) | copy-start | bytes 6291460
  7.2 132.6 %all-gather.2.cloned.1.call-start = ((), (), s32[]{:S(2)}) async-start(), calls=%async_computation | async-start | bytes 17825792 | tf_op jit(solution)/shard_map/all_gather | solution.py:22
  7.9 267.3 %all-reduce.2.cloned.1.call-start = ((), (), s32[]{:S(2)}) async-start(), calls=%async_computation.1 | async-start | bytes 786432 | tf_op jit(solution)/shard_map/psum | solution.py:28
  153.7 32.8 %copy-start.2 = (f32[128]{0:T(128)S(1)}, f32[128]{0:T(128)}, u32[]{:S(2)}) copy-start(f32[128]{0:T(128)} %param.11) | copy-start | bytes 1540
  276.0 0.7 copy-start.1
Sparse Core Ops, SparseCore 0:
  10.2 129.5 all-gather.1
  186.7 88.4 all-reduce.1
where the time goes:
time: 284 us; the launch traced here: 283 us
  waiting for transfers between devices  160 us (56%)
  matrix products  91.9 us (32%)
  local copies, waits for them, and re-layouts  16.3 us (6%)
  between operations  14.1 us (5%)
    psum x1, waiting for transfers between devices, per_device(): summed = lax.psum(proj, 'blk')  88.6 us
    all_gather x1, waiting for transfers between devices, per_device(): gathered = lax.all_gather(lower_vecs, 'blk', axis=0, tiled=True)  70.4 us
    dot_general x1, matrix products, per_device(): jnp.einsum('rkast,rsu->rkatu', dipole, upper_blocks, preferred_element_ty...  59 us
    dot_general x1, matrix products, per_device(): jnp.einsum('eatu,etl->aul', halves, lows, preferred_element_type=jnp.floa...  32.8 us
    gather x1, local copies, waits for them, and re-layouts, per_device(): lows = jnp.take(all_blocks, columns, axis=0)  13.9 us
  transfers between devices with their start and end apart: 2, of which 2 were waited for; matrix products, arithmetic and copies ran while one was open for 22% of the time, Pallas kernels for 0%

commit v1 on v0

--- a/solution.py
+++ b/solution.py
@@ -25,7 +25,7 @@
     proj = jnp.einsum("eatu,etl->aul", halves, lows, preferred_element_type=jnp.float32)
     share_rows = upper_count // group_size
     first_row = my_index * share_rows
-    summed = lax.psum(proj, "blk")
+    summed = jnp.sum(lax.all_gather(proj, "blk"), axis=0)
     own_share = lax.dynamic_slice_in_dim(summed, first_row, share_rows, 1)
     strength = jnp.sum(own_share * own_share, axis=0)
     energy_rows = lax.dynamic_slice_in_dim(upper_energy, first_row, share_rows, 0)

time: 284 us -> 258 us (0.908)
  waiting for transfers between devices: 160 us -> 132 us
    psum x1 -> x0, waiting for transfers between devices: 88.6 us -> none  [per_device(): summed = lax.psum(proj, 'blk')]
    all_gather x0 -> x1, waiting for transfers between devices: none -> 60.1 us  [per_device(): summed = jnp.sum(lax.all_gather(proj, 'blk'), axis=0)]
    reduce_sum x0 -> x1, other arithmetic: none -> 3.11 us  [per_device(): summed = jnp.sum(lax.all_gather(proj, 'blk'), axis=0)]
  transfers between devices with their start and end apart: 2 -> 2, of which waited for: 2 -> 2; matrix products, arithmetic and copies ran while one was open for 22% -> 24% of each run, Pallas kernels for 0% -> 0%
where the time goes in v1:
time: 258 us; the launch traced here: 257 us
  waiting for transfers between devices  132 us (51%)
  matrix products  92.2 us (36%)
  local copies, waits for them, and re-layouts  15.6 us (6%)
  between operations  14.1 us (5%)
  other arithmetic  3.83 us (1%)
    all_gather x1, waiting for transfers between devices, per_device(): gathered = lax.all_gather(lower_vecs, 'blk', axis=0, tiled=True)  70.8 us
    all_gather x1, waiting for transfers between devices, per_device(): summed = jnp.sum(lax.all_gather(proj, 'blk'), axis=0)  60.1 us
    dot_general x1, matrix products, per_device(): jnp.einsum('rkast,rsu->rkatu', dipole, upper_blocks, preferred_element_ty...  59.4 us
    dot_general x1, matrix products, per_device(): jnp.einsum('eatu,etl->aul', halves, lows, preferred_element_type=jnp.floa...  32.8 us
    gather x1, local copies, waits for them, and re-layouts, per_device(): lows = jnp.take(all_blocks, columns, axis=0)  14 us
  transfers between devices with their start and end apart: 2, of which 2 were waited for; matrix products, arithmetic and copies ran while one was open for 24% of the time, Pallas kernels for 0%

profile of v1, /device:TPU:0, one launch (start us, length us, event | category | flops | bytes accessed | tf_op | source)
XLA Modules:
  0.0 257.4 jit_solution(6576921972937563370)
XLA Ops:
  7.2 0.0 copy-start
  7.2 0.0 all-gather.4.cloned.1.call-start
  7.2 0.7 all-gather.4.cloned.1.call-update
  7.9 0.0 all-gather.6.cloned.1.call-start
  8.0 0.8 reshape.59
  8.7 0.8 reshape.57
  9.6 0.0 copy-done
  9.6 59.4 %convolution_convert_fusion = bf16[16,12,3,256,256]{4,3,2,1,0:T(8,128)(2,1)} fusion(bf16[16,12,3,256,256]{4,3,2,1,0:T(8,128)(2,1)} %param.6, bf16[16,256,256,1,1]{2,1,4,3,0:T(8,128)(2,1)S(1)} %bitcast.21), kind=kOutput, calls=%fused_computation.1 | convolution fusion | flops 19365101568 | bytes 153092096 | tf_op jit(solution)/shard_map/rkast,rsu->rkatu/dot_general | solution.py:14
  69.0 70.8 %all-gather.4.cloned.1.call-done = bf16[65536,128]{1,0:T(8,128)(2,1)} async-done(((bf16[4096,128]{1,0:T(8,128)(2,1)}), bf16[65536,128]{1,0:T(8,128)(2,1)}) %all-gather.4.cloned.1.call-update) | async-done | bytes 16777232 | tf_op jit(solution)/shard_map/all_gather | solution.py:22
  139.8 14.0 %gather_fusion = bf16[192,256,128]{2,1,0:T(8,128)(2,1)} fusion(bf16[256,256,128]{2,1,0:T(8,128)(2,1)} %bitcast.22, s32[1024]{0:T(1024)S(1)} %pad_clamp_fusion), kind=kCustom, calls=%fused_computation | custom fusion | bytes 25166592 | tf_op jit(solution)/shard_map/jit(_take)/gather | solution.py:24
  153.8 0.0 copy-start.3
  153.8 0.0 copy-start.2
  153.8 32.8 %fusion.5 = f32[3,256,128]{2,1,0:T(8,128)} fusion(bf16[192,3,256,256]{3,2,1,0:T(8,128)(2,1)} %bitcast.3, bf16[192,256,128]{2,1,0:T(8,128)(2,1)} %gather_fusion, pred[192]{0:T(512)(128)(4,1)S(1)} %compare_and_fusion), kind=kOutput, calls=%fused_computation.7 | convolution fusion | flops 9669967872 | bytes 88473792 | tf_op jit(solution)/shard_map/eatu,etl->aul/dot_general | solution.py:25
  186.6 0.0 all-gather.6.cloned.1.call-update
  186.6 0.0 copy-done.3
  186.6 0.1 dynamic_slice.7
  186.7 0.0 copy-done.2
  186.7 60.1 %all-gather.6.cloned.1.call-done = f32[48,256,128]{2,1,0:T(8,128)} async-done(((f32[3,256,128]{2,1,0:T(8,128)}), f32[48,256,128]{2,1,0:T(8,128)}) %all-gather.6.cloned.1.call-update) | async-done | bytes 6291472 | tf_op jit(solution)/shard_map/all_gather | solution.py:28
  246.8 3.1 %reduce_sum.18 = f32[3,256,128]{2,1,0:T(8,128)S(1)} reduce(f32[16,3,256,128]{3,2,1,0:T(8,128)} %bitcast.23, f32[]{:T(128)} %constant.12.clone.1), dimensions={0}, to_apply=%region_0.1 | reduce | flops 1474560 | bytes 6684676 | tf_op jit(solution)/shard_map/reduce_sum | solution.py:28
  249.9 0.0 copy-start.1
  249.9 0.7 fusion.9
  250.6 0.0 copy-done.1
  (5 shorter events, 0.0 us)
Async XLA Ops:
  7.2 2.4 copy-start
  7.2 132.6 %all-gather.4.cloned.1.call-start = ((), (), s32[]{:S(2)}) async-start(), calls=%async_computation | async-start | bytes 17825792 | tf_op jit(solution)/shard_map/all_gather | solution.py:22
  7.9 238.9 %all-gather.6.cloned.1.call-start = ((), (), s32[]{:S(2)}) async-start(), calls=%async_computation.1 | async-start | bytes 6684672 | tf_op jit(solution)/shard_map/all_gather | solution.py:28
  153.8 32.8 %copy-start.3 = (f32[256]{0:T(256)S(1)}, f32[256]{0:T(256)}, u32[]{:S(2)}) copy-start(f32[256]{0:T(256)} %param.10) | copy-start | bytes 3076
  153.8 32.9 %copy-start.2 = (f32[128]{0:T(128)S(1)}, f32[128]{0:T(128)}, u32[]{:S(2)}) copy-start(f32[128]{0:T(128)} %param.11) | copy-start | bytes 1540
  249.9 0.7 copy-start.1
Sparse Core Ops, SparseCore 0:
  10.2 129.5 all-gather.3
  186.7 60.0 all-gather.5
